TPU v7x, 256 devices: a whole 4x4x8 slice. The times are simulated.
256 devices in a mesh: req: 32 (over x, y, core), tp: 8 (over z).
Axes of the slice: x: 4, y: 4, z: 8, core: 2. Of those that a mesh axis runs over, the one named last changes fastest.
Arguments:
- queries: bfloat16 [4096, 8192], P('req', 'tp'), may hold values from -80 to 80
- incoming_key_value: bfloat16 [2, 4096, 1024], P(None, 'req', 'tp'), may hold values from -4 to 4
- key_value_pages: bfloat16 [16384, 32, 2, 1024], P('req', None, None, 'tp'), may hold values from -4 to 4
- page_request_home: int32 [16384], P('req'), may hold values from 0 to 16383, as said below
- lengths: int32 [1024], P('req'), may hold values from 1 to 512, 262144 in all
- request_adapter_index: int32 [1024], P('req'), may hold values from 0 to 63
- adapter_storage_slot: int32 [64], replicated, may hold values from 0 to 63, each once
- adapter_down_factor: bfloat16 [64, 8192, 64], P('req', 'tp'), may hold values from -0.25 to 0.25
- adapter_up_factor: bfloat16 [64, 64, 8192], P('req'), may hold values from -0.75 to 0.75
- output_projection_weight: bfloat16 [8192, 8192], P('tp', 'req'), may hold values from -0.75 to 0.75
Outputs:
- attn_out: bfloat16 [4096, 8192], P('tp', 'req')
Inputs may be any that keep to these rules, and one draw needn't show every extreme that they name: `page_request_home`: each value once. Pages p with p // 512 = a hold pages of requests i with i // 32 = b, b != a, for at most 2 pages p for every pair a, b; in every draw some a holds exactly 2 pages of every b != a.
All inputs are finite; a program needn't handle non-finite values. No bound on the sum of `lengths` on one device may be relied on, other than what follows from the above.
Results may differ from a plain program's by a relative error of at most 0.0058.
Values may be sent and summed in bfloat16 or wider, within the bound.
A program may use at most 128 MiB of HBM per device.

v0:
```python
import math
import jax
import jax.numpy as jnp
from jax import lax
from jax.sharding import PartitionSpec as P

QUERY_HEADS = 64
KEY_VALUE_HEADS = 8
HEAD_WIDTH = 128
STEP_COUNT = 4
PAGE_LENGTH = 32
MAXP = 16
CAP = 2


def relocate(key_value_pages, page_request_home, my_req, req_count):
    per_dev = key_value_pages.shape[0]
    destination = page_request_home // per_dev
    remote = destination != my_req
    matches = (destination[:, None] == jnp.arange(req_count, dtype=jnp.int32)[None, :]) & remote[
        :, None
    ]
    before = jnp.cumsum(matches.astype(jnp.int32), axis=0) - 1
    placing = jnp.sum(jnp.where(matches, before, 0), axis=1)
    target = jnp.where(remote, destination * CAP + placing, req_count * CAP)
    page_numbers = jnp.arange(per_dev, dtype=jnp.int32)
    out_match = target[:, None] == jnp.arange(req_count * CAP, dtype=jnp.int32)[None, :]
    filled = jnp.any(out_match, axis=0)
    out_source = jnp.sum(jnp.where(out_match, page_numbers[:, None], 0), axis=0)
    out_label = jnp.sum(jnp.where(out_match, page_request_home[:, None], 0), axis=0)
    picked = jnp.take(key_value_pages, out_source, axis=0)
    outbox = jnp.where(filled[:, None, None, None], picked, jnp.zeros((), key_value_pages.dtype))
    labels = jnp.where(filled, out_label, -1)
    inbox_pages, arrived = (
        lax.all_to_all(outbox, "req", split_axis=0, concat_axis=0, tiled=True),
        lax.all_to_all(labels, "req", split_axis=0, concat_axis=0, tiled=True),
    )
    own_label = jnp.where(remote, -1, page_request_home - my_req * per_dev)
    in_label = jnp.where(arrived >= 0, arrived - my_req * per_dev, -1)
    candidate_label = jnp.concatenate([own_label, in_label], axis=0)
    candidates = jnp.concatenate([key_value_pages, inbox_pages], axis=0)
    candidate_numbers = jnp.arange(candidate_label.shape[0], dtype=jnp.int32)
    slot_match = candidate_label[:, None] == page_numbers[None, :]
    slot_source = jnp.sum(jnp.where(slot_match, candidate_numbers[:, None], 0), axis=0)
    return jnp.take(candidates, slot_source, axis=0)


def attend(queries, incoming_key_value, cache_pages, lengths):
    heads_kv = cache_pages.shape[-1] // HEAD_WIDTH
    query_group_count = QUERY_HEADS // KEY_VALUE_HEADS
    requests = lengths.shape[0]
    cache_extent = MAXP * PAGE_LENGTH
    score_scale = 1.0 / math.sqrt(HEAD_WIDTH)
    stored_entries = cache_pages.reshape(requests, cache_extent, 2, heads_kv, HEAD_WIDTH)
    fresh_key_value = incoming_key_value.reshape(2, requests, STEP_COUNT, heads_kv, HEAD_WIDTH)
    query_vectors = queries.reshape(requests, STEP_COUNT, heads_kv, query_group_count, HEAD_WIDTH)
    old_scores = (
        jnp.einsum(
            "rsgqd,rlgd->rgqsl",
            query_vectors,
            stored_entries[:, :, 0],
            preferred_element_type=jnp.float32,
        )
        * score_scale
    )
    new_scores = (
        jnp.einsum(
            "rsgqd,rtgd->rgqst",
            query_vectors,
            fresh_key_value[0],
            preferred_element_type=jnp.float32,
        )
        * score_scale
    )
    keep_old = jnp.arange(cache_extent, dtype=jnp.int32)[None, :] < lengths[:, None]
    keep_new = jnp.arange(STEP_COUNT)[None, :] <= jnp.arange(STEP_COUNT)[:, None]
    old_scores = jnp.where(keep_old[:, None, None, None, :], old_scores, -jnp.inf)
    new_scores = jnp.where(keep_new[None, None, None], new_scores, -jnp.inf)
    row_top = jnp.maximum(jnp.max(old_scores, axis=-1), jnp.max(new_scores, axis=-1))
    old_weights = jnp.exp(old_scores - row_top[..., None])
    new_weights = jnp.exp(new_scores - row_top[..., None])
    totals = jnp.sum(old_weights, axis=-1) + jnp.sum(new_weights, axis=-1)
    old_probs = (old_weights / totals[..., None]).astype(jnp.bfloat16)
    new_probs = (new_weights / totals[..., None]).astype(jnp.bfloat16)
    attention_mixed_output = jnp.einsum(
        "rgqsl,rlgd->rsgqd", old_probs, stored_entries[:, :, 1], preferred_element_type=jnp.float32
    )
    attention_mixed_output = attention_mixed_output + jnp.einsum(
        "rgqst,rtgd->rsgqd", new_probs, fresh_key_value[1], preferred_element_type=jnp.float32
    )
    return attention_mixed_output.astype(jnp.bfloat16).reshape(
        requests * STEP_COUNT, heads_kv * query_group_count * HEAD_WIDTH
    )


def on_device(
    queries,
    incoming_key_value,
    key_value_pages,
    page_request_home,
    lengths,
    request_adapter_index,
    adapter_storage_slot,
    adapter_down_factor,
    adapter_up_factor,
    output_projection_weight,
):
    req_count = lax.axis_size("req")
    tp_count = lax.axis_size("tp")
    my_req = lax.axis_index("req")
    my_lane = lax.axis_index("tp")
    cache_pages = relocate(key_value_pages, page_request_home, my_req, req_count)
    attention_mixed_output = attend(queries, incoming_key_value, cache_pages, lengths)
    own_tokens = attention_mixed_output.shape[0]
    everyone, adapters = (
        lax.all_gather(attention_mixed_output, "req", axis=0, tiled=True),
        lax.all_gather(request_adapter_index, "req", axis=0, tiled=True),
    )
    slot_count = adapter_storage_slot.shape[0]
    match_table = adapters[:, None] == jnp.arange(slot_count, dtype=jnp.int32)[None, :]
    req_slot = jnp.sum(jnp.where(match_table, adapter_storage_slot[None, :], 0), axis=1)
    token_slot = jnp.repeat(req_slot, STEP_COUNT)
    block_rows = everyone.shape[0] // tp_count
    plain_output_rows = lax.psum_scatter(
        jnp.dot(everyone, output_projection_weight, preferred_element_type=jnp.float32),
        "tp",
        scatter_dimension=0,
        tiled=True,
    )
    gathered_down_factors = lax.all_gather(adapter_down_factor, "req", axis=0, tiled=True)
    local_reduced_rows = jnp.einsum(
        "td,adr->tar",
        attention_mixed_output,
        gathered_down_factors,
        preferred_element_type=jnp.float32,
    )
    own_slot = lax.dynamic_slice_in_dim(token_slot, my_req * own_tokens, own_tokens)
    selected_pages = own_slot[:, None] == jnp.arange(slot_count, dtype=jnp.int32)[None, :]
    adapter_partial = jnp.sum(
        jnp.where(selected_pages[:, :, None], local_reduced_rows, 0.0), axis=1
    )
    distributed_terms = lax.all_gather(adapter_partial, "req", axis=0, tiled=True)
    low_rows = lax.psum_scatter(distributed_terms, "tp", scatter_dimension=0, tiled=True)
    up_factor_columns = lax.all_to_all(
        adapter_up_factor, "req", split_axis=2, concat_axis=0, tiled=True
    )
    low_bf = low_rows.astype(jnp.bfloat16)
    block_slot = lax.dynamic_slice_in_dim(token_slot, my_lane * block_rows, block_rows)
    selector = (block_slot[:, None] == jnp.arange(slot_count, dtype=jnp.int32)[None, :]).astype(
        jnp.bfloat16
    )
    expanded = (selector[:, :, None] * low_bf[:, None, :]).reshape(
        block_rows, slot_count * up_factor_columns.shape[1]
    )
    adapter_output_rows = jnp.dot(
        expanded,
        up_factor_columns.reshape(
            slot_count * up_factor_columns.shape[1], up_factor_columns.shape[2]
        ),
        preferred_element_type=jnp.float32,
    )
    return (plain_output_rows + adapter_output_rows).astype(jnp.bfloat16)


def solution(mesh):
    return jax.shard_map(
        on_device,
        mesh=mesh,
        in_specs=(
            P("req", "tp"),
            P(None, "req", "tp"),
            P("req", None, None, "tp"),
            P("req"),
            P("req"),
            P("req"),
            P(),
            P("req", "tp", None),
            P("req", None, None),
            P("tp", "req"),
        ),
        out_specs=P("tp", "req"),
        check_vma=False,
    )
```

profile of v0, /device:TPU:1, one launch (start us, length us, event | category | flops | bytes accessed | tf_op | source)
XLA Modules:
  0.0 376.8 jit_solution(3903700811539374699)
XLA Ops:
  11.2 8.6 %all-to-all-start = ((s32[32,2,1]{1,2,0:T(1,128)}), s32[32,2,1]{1,2,0:T(1,128)S(1)}, u32[]{:S(2)}, u32[]{:S(2)}) async-start(s32[32,2,1]{1,2,0:T(1,128)} %bitcast.3), calls=%async_computation | async-start | bytes 32768 | tf_op jit(solution)/shard_map/all_to_all | solution.py:36
  20.8 6.0 %gather_fusion = bf16[64,32,2,128]{3,2,1,0:T(2,128)(2,1)S(1)} fusion(bf16[512,32,2,128]{3,2,1,0:T(2,128)(2,1)} %param.12, s32[1024]{0:T(1024)S(1)} %pad_clamp_fusion.1), kind=kCustom, calls=%fused_computation | custom fusion | bytes 2097408 | tf_op jit(solution)/shard_map/jit(_take)/gather | solution.py:31
  29.8 13.7 %all-reduce = s32[1024]{0:T(1024)S(1)} all-reduce(s32[1024]{0:T(1024)S(1)} %dynamic-update-slice), channel_id=1, replica_groups=mesh['req'=32,'tp'=8] {'req'}, use_global_device_ids=true, to_apply=%add | all-reduce | flops 1024 | bytes 8192
  47.1 2.4 broadcast_select_fusion.2
  50.0 7.1 %all-to-all-start.1 = ((bf16[64,32,2,128]{3,2,1,0:T(2,128)(2,1)}), bf16[64,32,2,128]{3,2,1,0:T(2,128)(2,1)S(1)}, u32[]{:S(2)}, u32[]{:S(2)}) async-start(bf16[64,32,2,128]{3,2,1,0:T(2,128)(2,1)} %broadcast_select_fusion.2), calls=%async_computation.1 | async-start | bytes 2097152 | tf_op jit(solution)/shard_map/all_to_all | solution.py:35
  58.0 24.3 %all-to-all-done.1 = bf16[64,32,2,128]{3,2,1,0:T(2,128)(2,1)S(1)} async-done(((bf16[64,32,2,128]{3,2,1,0:T(2,128)(2,1)}), bf16[64,32,2,128]{3,2,1,0:T(2,128)(2,1)S(1)}, u32[]{:S(2)}, u32[]{:S(2)}) %all-to-all-start.1) | async-done | bytes 1048608 | tf_op jit(solution)/shard_map/all_to_all | solution.py:35
  82.3 25.9 %pad_maximum_fusion = bf16[576,32,2,128]{3,2,1,0:T(2,128)(2,1)} fusion(bf16[64,32,2,128]{3,2,1,0:T(2,128)(2,1)S(1)} %all-to-all-done.1, bf16[512,32,2,128]{3,2,1,0:T(2,128)(2,1)} %param.12), kind=kLoop, calls=%fused_computation.2 | loop fusion | flops 4718592 | bytes 18874368 | tf_op jit(solution)/shard_map/concatenate | solution.py:41
  108.2 30.0 %gather_fusion.1 = bf16[512,32,2,128]{3,2,1,0:T(2,128)(2,1)} fusion(bf16[576,32,2,128]{3,2,1,0:T(2,128)(2,1)} %pad_maximum_fusion, s32[1024]{0:T(1024)S(1)} %pad_clamp_fusion), kind=kCustom, calls=%fused_computation.1 | custom fusion | bytes 16779264 | tf_op jit(solution)/shard_map/jit(_take)/gather | solution.py:45
  138.2 7.9 %copy.25 = bf16[512,32,2,128]{3,1,0,2:T(8,128)(2,1)} copy(bf16[512,32,2,128]{3,2,1,0:T(2,128)(2,1)} %gather_fusion.1) | data formatting | bytes 16777216 | tf_op jit(solution)/shard_map/jit(_take)/gather | solution.py:45
  146.1 5.3 %broadcast_select_fusion = bf16[32,512,2,1,128]{4,1,0,3,2:T(8,128)(2,1)S(1)} fusion(bf16[32,512,2,1,128]{4,1,0,3,2:T(8,128)(2,1)} %bitcast.129, pred[32,512]{1,0:T(8,128)(4,1)S(1)} %broadcast_in_dim.174), kind=kLoop, calls=%fused_computation.3 | loop fusion | flops 4194304 | bytes 16793600 | tf_op jit(solution)/shard_map/jit(_take)/select_n | solution.py:45
  151.5 1.6 bitcast_reduce_fusion
  155.8 5.8 %fusion.30 = f32[128,4096]{0,1:S(1)} fusion(bf16[1024,4096]{0,1:T(8,128)(2,1)} %bitcast.132, bf16[16,8,8,128]{3,2,1,0:T(8,128)(2,1)S(1)} %bitcast.137), kind=kOutput, calls=%fused_computation.85 | convolution fusion | flops 1073741824 | bytes 10747904
  163.3 45.8 %all-gather.8.cloned.1.call-done = f32[4096,64]{0,1:T(8,128)} async-done(((f32[128,64]{0,1:T(8,128)}), f32[4096,64]{0,1:T(8,128)}) %all-gather.8.cloned.1.call-update) | async-done | bytes 1048592 | tf_op jit(solution)/shard_map/all_gather | solution.py:142
  209.5 59.6 %all-gather.4.cloned.1.call-done = bf16[4096,1024]{1,0:T(8,128)(2,1)} async-done(((bf16[128,1024]{1,0:T(8,128)(2,1)}), bf16[4096,1024]{1,0:T(8,128)(2,1)}) %all-gather.4.cloned.1.call-update) | async-done | bytes 8388624 | tf_op jit(solution)/shard_map/all_gather | solution.py:116
  269.0 7.7 %fusion.33 = f32[4096,256]{1,0:T(8,128)} fusion(bf16[4096,1024]{1,0:T(8,128)(2,1)} %all-gather.4.cloned.1.call-done, bf16[1024,256]{1,0:T(8,128)(2,1)S(1)} %copy-done), kind=kOutput, calls=%fused_computation.88 | convolution fusion | flops 2147483648 | bytes 13107200 | tf_op jit(solution)/shard_map/dot_general | solution.py:125
  278.3 6.9 %copy.26 = bf16[2,64,8192]{1,0,2:T(2,128)(2,1)} copy(bf16[2,64,8192]{2,1,0:T(8,128)(2,1)S(1)} %copy-done.1) | data formatting | bytes 4194304 | tf_op args[8]
  285.2 9.8 %reshape.331 = bf16[32,2,16384]{2,1,0:T(2,128)(2,1)} reshape(bf16[8192,2,64]{2,1,0:T(2,128)(2,1)} %bitcast.131) | data formatting | bytes 4194304
  295.0 5.5 %all-to-all-start.2 = ((bf16[32,2,16384]{2,1,0:T(2,128)(2,1)}), bf16[32,2,16384]{2,1,0:T(2,128)(2,1)S(1)}, u32[]{:S(2)}, u32[]{:S(2)}) async-start(bf16[32,2,16384]{2,1,0:T(2,128)(2,1)} %reshape.331), calls=%async_computation.4 | async-start | bytes 4194304 | tf_op jit(solution)/shard_map/all_to_all | solution.py:144
  300.6 28.2 %all-to-all-done.2 = bf16[32,2,16384]{2,1,0:T(2,128)(2,1)S(1)} async-done(((bf16[32,2,16384]{2,1,0:T(2,128)(2,1)}), bf16[32,2,16384]{2,1,0:T(2,128)(2,1)S(1)}, u32[]{:S(2)}, u32[]{:S(2)}) %all-to-all-start.2) | async-done | bytes 2097184 | tf_op jit(solution)/shard_map/all_to_all | solution.py:144
  328.9 4.0 %reshape.332 = bf16[8192,2,64]{2,1,0:T(2,128)(2,1)} reshape(bf16[32,2,16384]{2,1,0:T(2,128)(2,1)S(1)} %all-to-all-done.2) | data formatting | bytes 4194304
  332.9 9.3 %copy.34 = bf16[2,64,32,256]{3,1,0,2:T(8,128)(2,1)S(1)} copy(bf16[2,64,32,256]{1,0,3,2:T(2,128)(2,1)} %bitcast.130) | data formatting | bytes 4194304 | tf_op jit(solution)/shard_map/all_to_all | solution.py:144
  343.1 2.2 broadcast_multiply_fusion
  345.3 20.7 %reduce-scatter.3.cloned.1.call-done = f32[512,256]{1,0:T(8,128)} async-done(((f32[4096,256]{1,0:T(8,128)}), f32[512,256]{1,0:T(8,128)}) %reduce-scatter.3.cloned.1.call-update) | async-done | bytes 524304 | tf_op jit(solution)/shard_map/reduce_scatter | solution.py:124
  366.0 4.3 %fusion.5 = bf16[512,256]{1,0:T(8,128)(2,1)} fusion(f32[512,256]{1,0:T(8,128)} %reduce-scatter.3.cloned.1.call-done, bf16[512,4096]{0,1:T(8,128)(2,1)} %bitcast.134, bf16[4096,256]{1,0:T(8,128)(2,1)S(1)} %bitcast.135), kind=kOutput, calls=%fused_computation.21 | convolution fusion | flops 1074003968 | bytes 7077888 | tf_op jit(solution)/shard_map/dot_general | solution.py:155
  (66 shorter events, 20.1 us)
Async XLA Ops:
  6.5 262.5 %copy-start = (bf16[1024,256]{1,0:T(8,128)(2,1)S(1)}, bf16[1024,256]{1,0:T(8,128)(2,1)}, u32[]{:S(2)}) copy-start(bf16[1024,256]{1,0:T(8,128)(2,1)} %param.19) | copy-start | bytes 1572868
  6.5 149.2 %all-gather.6.cloned.1.call-start = ((), (), s32[]{:S(2)}) async-start(), calls=%async_computation.7 | async-start | bytes 8650752 | tf_op jit(solution)/shard_map/all_gather | solution.py:130
  11.2 38.8 %all-to-all-start = ((s32[32,2,1]{1,2,0:T(1,128)}), s32[32,2,1]{1,2,0:T(1,128)S(1)}, u32[]{:S(2)}, u32[]{:S(2)}) async-start(s32[32,2,1]{1,2,0:T(1,128)} %bitcast.3), calls=%async_computation | async-start | bytes 32768 | tf_op jit(solution)/shard_map/all_to_all | solution.py:36
  50.0 32.3 %all-to-all-start.1 = ((bf16[64,32,2,128]{3,2,1,0:T(2,128)(2,1)}), bf16[64,32,2,128]{3,2,1,0:T(2,128)(2,1)S(1)}, u32[]{:S(2)}, u32[]{:S(2)}) async-start(bf16[64,32,2,128]{3,2,1,0:T(2,128)(2,1)} %broadcast_select_fusion.2), calls=%async_computation.1 | async-start | bytes 2097152 | tf_op jit(solution)/shard_map/all_to_all | solution.py:35
  57.2 152.0 %all-gather.8.cloned.1.call-start = ((), (), s32[]{:S(2)}) async-start(), calls=%async_computation.8 | async-start | bytes 1081344 | tf_op jit(solution)/shard_map/all_gather | solution.py:142
  162.5 106.6 %all-gather.4.cloned.1.call-start = ((), (), s32[]{:S(2)}) async-start(), calls=%async_computation.5 | async-start | bytes 8650752 | tf_op jit(solution)/shard_map/all_gather | solution.py:116
  163.3 178.9 %reduce-scatter.5.cloned.1.call-start = ((), (), s32[]{:S(2)}) async-start(), calls=%async_computation.9 | async-start | bytes 1179648 | tf_op jit(solution)/shard_map/reduce_scatter | solution.py:143
  209.2 156.8 %reduce-scatter.3.cloned.1.call-start = ((), (), s32[]{:S(2)}) async-start(), calls=%async_computation.6 | async-start | bytes 4718592 | tf_op jit(solution)/shard_map/reduce_scatter | solution.py:124
  276.7 1.6 copy-start.1
  295.0 33.8 %all-to-all-start.2 = ((bf16[32,2,16384]{2,1,0:T(2,128)(2,1)}), bf16[32,2,16384]{2,1,0:T(2,128)(2,1)S(1)}, u32[]{:S(2)}, u32[]{:S(2)}) async-start(bf16[32,2,16384]{2,1,0:T(2,128)(2,1)} %reshape.331), calls=%async_computation.4 | async-start | bytes 4194304 | tf_op jit(solution)/shard_map/all_to_all | solution.py:144
Sparse Core Ops, SparseCore 0:
  9.9 72.5 all-gather.5
  162.6 46.5 all-gather.7
  211.7 57.2 all-gather.3
  271.4 33.2 reduce-scatter.4
  307.1 58.8 reduce-scatter.2
where the time goes:
time: 378 us; the launch traced here: 377 us
  waiting for transfers between devices  179 us (47%)
  local copies, waits for them, and re-layouts  82.3 us (22%)
  other arithmetic  43.6 us (12%)
  matrix products  22.1 us (6%)
  starting transfers between devices  21.6 us (6%)
  between operations  14.1 us (4%)
  blocking collectives  13.7 us (4%)
    all_gather x1, waiting for transfers between devices, on_device(): lax.all_gather(attention_mixed_output, 'req', axis=0, tiled=True)  59.6 us
    all_gather x1, waiting for transfers between devices, on_device(): lax.all_gather(adapter_partial, 'req', axis=0, tiled=True)  45.8 us
    gather x2, local copies, waits for them, and re-layouts, relocate(): return jnp.take(candidates, slot_source, axis=0)  37.9 us
    all_to_all x1, waiting for transfers between devices, on_device(): lax.all_to_all(adapter_up_factor, 'req', split_axis=2, concat_axis=0, til...  28.2 us
    unnamed x12, local copies, waits for them, and re-layouts  26.2 us
    concatenate x1, other arithmetic, relocate(): candidates = jnp.concatenate([key_value_pages, inbox_pages], axis=0)  25.9 us
    all_to_all x1, waiting for transfers between devices, relocate(): lax.all_to_all(outbox, 'req', split_axis=0, concat_axis=0, tiled=True)  24.3 us
    reduce_scatter x1, waiting for transfers between devices, on_device(): lax.psum_scatter(jnp.dot(everyone, output_projection_weight, preferred_el...  20.7 us
  transfers between devices with their start and end apart: 8, of which 5 were waited for; matrix products, arithmetic and copies ran while one was open for 36% of the time, Pallas kernels for 0%

commit v1 on v0

--- a/solution.py
+++ b/solution.py
@@ -139,7 +139,9 @@
     adapter_partial = jnp.sum(
         jnp.where(selected_pages[:, :, None], local_reduced_rows, 0.0), axis=1
     )
-    distributed_terms = lax.all_gather(adapter_partial, "req", axis=0, tiled=True)
+    distributed_terms = jnp.concatenate(
+        lax.all_to_all(jnp.stack([adapter_partial] * lax.axis_size("req")), "req", 0, 0), axis=0
+    )
     low_rows = lax.psum_scatter(distributed_terms, "tp", scatter_dimension=0, tiled=True)
     up_factor_columns = lax.all_to_all(
         adapter_up_factor, "req", split_axis=2, concat_axis=0, tiled=True

time: 378 us -> 303 us (0.80)
  waiting for transfers between devices: 179 us -> 85.4 us
  blocking collectives: 13.7 us -> 36 us
    all_gather x1 -> x0, waiting for transfers between devices: 45.8 us -> none  [on_device(): lax.all_gather(adapter_partial, 'req', axis=0, tiled=True)]
    all_gather x1, waiting for transfers between devices: 59.6 us -> 16.5 us  [on_device(): lax.all_gather(attention_mixed_output, 'req', axis=0, tiled=True)]
    all_to_all x0 -> x1, blocking collectives: none -> 24.9 us  [on_device(): lax.all_to_all(jnp.stack([adapter_partial] * lax.axis_size('req')), 'req'...]
    all_to_all x1, waiting for transfers between devices: 24.3 us -> 16 us  [relocate(): lax.all_to_all(outbox, 'req', split_axis=0, concat_axis=0, tiled=True)]
    unnamed x12 -> x20, local copies, waits for them, and re-layouts: 26.2 us -> 24.8 us
  transfers between devices with their start and end apart: 8 -> 7, of which waited for: 5 -> 4; matrix products, arithmetic and copies ran while one was open for 36% -> 46% of each run, Pallas kernels for 0% -> 0%
where the time goes in v1:
time: 303 us; the launch traced here: 302 us
  waiting for transfers between devices  85.4 us (28%)
  local copies, waits for them, and re-layouts  82.2 us (27%)
  other arithmetic  41.6 us (14%)
  blocking collectives  36 us (12%)
  matrix products  22.4 us (7%)
  starting transfers between devices  20.6 us (7%)
  between operations  14 us (5%)
    gather x2, local copies, waits for them, and re-layouts, relocate(): return jnp.take(candidates, slot_source, axis=0)  37.9 us
    all_to_all x1, waiting for transfers between devices, on_device(): lax.all_to_all(adapter_up_factor, 'req', split_axis=2, concat_axis=0, til...  28.2 us
    concatenate x1, other arithmetic, relocate(): candidates = jnp.concatenate([key_value_pages, inbox_pages], axis=0)  25.9 us
    all_to_all x1, blocking collectives, on_device(): lax.all_to_all(jnp.stack([adapter_partial] * lax.axis_size('req')), 'req'...  24.9 us
    unnamed x20, local copies, waits for them, and re-layouts  24.8 us
    reduce_scatter x1, waiting for transfers between devices, on_device(): lax.psum_scatter(jnp.dot(everyone, output_projection_weight, preferred_el...  23.8 us
    all_gather x1, waiting for transfers between devices, on_device(): lax.all_gather(attention_mixed_output, 'req', axis=0, tiled=True)  16.5 us
    all_to_all x1, waiting for transfers between devices, relocate(): lax.all_to_all(outbox, 'req', split_axis=0, concat_axis=0, tiled=True)  16 us
  transfers between devices with their start and end apart: 7, of which 4 were waited for; matrix products, arithmetic and copies ran while one was open for 46% of the time, Pallas kernels for 0%

profile of v1, /device:TPU:1, one launch (start us, length us, event | category | flops | bytes accessed | tf_op | source)
XLA Modules:
  0.0 302.2 jit_solution(6709512376872074682)
XLA Ops:
  11.2 8.6 %all-to-all-start = ((s32[32,2,1]{1,2,0:T(1,128)}), s32[32,2,1]{1,2,0:T(1,128)S(1)}, u32[]{:S(2)}, u32[]{:S(2)}) async-start(s32[32,2,1]{1,2,0:T(1,128)} %bitcast.3), calls=%async_computation | async-start | bytes 32768 | tf_op jit(solution)/shard_map/all_to_all | solution.py:36
  20.8 6.0 %gather_fusion = bf16[64,32,2,128]{3,2,1,0:T(2,128)(2,1)S(1)} fusion(bf16[512,32,2,128]{3,2,1,0:T(2,128)(2,1)} %param.12, s32[1024]{0:T(1024)S(1)} %pad_clamp_fusion.1), kind=kCustom, calls=%fused_computation | custom fusion | bytes 2097408 | tf_op jit(solution)/shard_map/jit(_take)/gather | solution.py:31
  27.7 2.4 broadcast_select_fusion.2
  31.3 7.4 %all-to-all-start.1 = ((bf16[64,32,2,128]{3,2,1,0:T(2,128)(2,1)}), bf16[64,32,2,128]{3,2,1,0:T(2,128)(2,1)S(1)}, u32[]{:S(2)}, u32[]{:S(2)}) async-start(bf16[64,32,2,128]{3,2,1,0:T(2,128)(2,1)} %broadcast_select_fusion.2), calls=%async_computation.1 | async-start | bytes 2097152 | tf_op jit(solution)/shard_map/all_to_all | solution.py:35
  39.9 16.0 %all-to-all-done.1 = bf16[64,32,2,128]{3,2,1,0:T(2,128)(2,1)S(1)} async-done(((bf16[64,32,2,128]{3,2,1,0:T(2,128)(2,1)}), bf16[64,32,2,128]{3,2,1,0:T(2,128)(2,1)S(1)}, u32[]{:S(2)}, u32[]{:S(2)}) %all-to-all-start.1) | async-done | bytes 1048608 | tf_op jit(solution)/shard_map/all_to_all | solution.py:35
  55.9 25.9 %pad_maximum_fusion = bf16[576,32,2,128]{3,2,1,0:T(2,128)(2,1)} fusion(bf16[64,32,2,128]{3,2,1,0:T(2,128)(2,1)S(1)} %all-to-all-done.1, bf16[512,32,2,128]{3,2,1,0:T(2,128)(2,1)} %param.12), kind=kLoop, calls=%fused_computation.2 | loop fusion | flops 4718592 | bytes 18874368 | tf_op jit(solution)/shard_map/concatenate | solution.py:41
  81.7 30.0 %gather_fusion.1 = bf16[512,32,2,128]{3,2,1,0:T(2,128)(2,1)} fusion(bf16[576,32,2,128]{3,2,1,0:T(2,128)(2,1)} %pad_maximum_fusion, s32[1024]{0:T(1024)S(1)} %pad_clamp_fusion), kind=kCustom, calls=%fused_computation.1 | custom fusion | bytes 16779264 | tf_op jit(solution)/shard_map/jit(_take)/gather | solution.py:45
  111.8 7.9 %copy.32 = bf16[512,32,2,128]{3,1,0,2:T(8,128)(2,1)} copy(bf16[512,32,2,128]{3,2,1,0:T(2,128)(2,1)} %gather_fusion.1) | data formatting | bytes 16777216 | tf_op jit(solution)/shard_map/jit(_take)/gather | solution.py:45
  119.7 5.3 %broadcast_select_fusion = bf16[32,512,2,1,128]{4,1,0,3,2:T(8,128)(2,1)S(1)} fusion(bf16[32,512,2,1,128]{4,1,0,3,2:T(8,128)(2,1)} %bitcast.134, pred[32,512]{1,0:T(8,128)(4,1)S(1)} %broadcast_in_dim.174), kind=kLoop, calls=%fused_computation.3 | loop fusion | flops 4194304 | bytes 16793600 | tf_op jit(solution)/shard_map/jit(_take)/select_n | solution.py:45
  125.0 1.6 bitcast_reduce_fusion
  131.5 11.0 %all-reduce = s32[1024]{0:T(1024)S(1)} all-reduce(s32[1024]{0:T(1024)S(1)} %dynamic-update-slice), channel_id=1, replica_groups=mesh['req'=32,'tp'=8] {'req'}, use_global_device_ids=true, to_apply=%add | all-reduce | flops 1024 | bytes 8192
  143.3 6.1 %fusion.30 = f32[128,4096]{0,1:S(1)} fusion(bf16[1024,4096]{0,1:T(8,128)(2,1)} %bitcast.137, bf16[16,8,8,128]{3,2,1,0:T(8,128)(2,1)S(1)} %bitcast.143), kind=kOutput, calls=%fused_computation.86 | convolution fusion | flops 1073741824 | bytes 10747904
  149.7 24.9 %all_to_all.31 = f32[32,128,64]{1,2,0:T(8,128)S(1)} all-to-all(f32[32,128,64]{1,2,0:T(8,128)S(1)} %stack.2), channel_id=1, replica_groups=mesh['req'=32,'tp'=8] {'req'}, dimensions={0} | all-to-all | bytes 2097152 | tf_op jit(solution)/shard_map/all_to_all | solution.py:143
  175.9 16.5 %all-gather.3.cloned.1.call-done = bf16[4096,1024]{1,0:T(8,128)(2,1)} async-done(((bf16[128,1024]{1,0:T(8,128)(2,1)}), bf16[4096,1024]{1,0:T(8,128)(2,1)}) %all-gather.3.cloned.1.call-update) | async-done | bytes 8388624 | tf_op jit(solution)/shard_map/all_gather | solution.py:116
  192.4 7.7 %fusion.33 = f32[4096,256]{1,0:T(8,128)} fusion(bf16[4096,1024]{1,0:T(8,128)(2,1)} %all-gather.3.cloned.1.call-done, bf16[1024,256]{1,0:T(8,128)(2,1)S(1)} %copy-done), kind=kOutput, calls=%fused_computation.89 | convolution fusion | flops 2147483648 | bytes 13107200 | tf_op jit(solution)/shard_map/dot_general | solution.py:125
  201.7 6.9 %copy.34 = bf16[2,64,8192]{1,0,2:T(2,128)(2,1)} copy(bf16[2,64,8192]{2,1,0:T(8,128)(2,1)S(1)} %copy-done.1) | data formatting | bytes 4194304 | tf_op args[8]
  208.6 9.8 %reshape.337 = bf16[32,2,16384]{2,1,0:T(2,128)(2,1)} reshape(bf16[8192,2,64]{2,1,0:T(2,128)(2,1)} %bitcast.136) | data formatting | bytes 4194304
  218.4 4.3 %all-to-all-start.3 = ((bf16[32,2,16384]{2,1,0:T(2,128)(2,1)}), bf16[32,2,16384]{2,1,0:T(2,128)(2,1)S(1)}, u32[]{:S(2)}, u32[]{:S(2)}) async-start(bf16[32,2,16384]{2,1,0:T(2,128)(2,1)} %reshape.337), calls=%async_computation.5 | async-start | bytes 4194304 | tf_op jit(solution)/shard_map/all_to_all | solution.py:146
  222.8 28.2 %all-to-all-done.3 = bf16[32,2,16384]{2,1,0:T(2,128)(2,1)S(1)} async-done(((bf16[32,2,16384]{2,1,0:T(2,128)(2,1)}), bf16[32,2,16384]{2,1,0:T(2,128)(2,1)S(1)}, u32[]{:S(2)}, u32[]{:S(2)}) %all-to-all-start.3) | async-done | bytes 2097184 | tf_op jit(solution)/shard_map/all_to_all | solution.py:146
  251.0 4.0 %reshape.338 = bf16[8192,2,64]{2,1,0:T(2,128)(2,1)} reshape(bf16[32,2,16384]{2,1,0:T(2,128)(2,1)S(1)} %all-to-all-done.3) | data formatting | bytes 4194304
  255.0 9.3 %copy.42 = bf16[2,64,32,256]{3,1,0,2:T(8,128)(2,1)S(1)} copy(bf16[2,64,32,256]{1,0,3,2:T(2,128)(2,1)} %bitcast.135) | data formatting | bytes 4194304 | tf_op jit(solution)/shard_map/all_to_all | solution.py:146
  265.3 2.2 broadcast_multiply_fusion
  267.5 23.8 %reduce-scatter.3.cloned.1.call-done = f32[512,256]{1,0:T(8,128)} async-done(((f32[4096,256]{1,0:T(8,128)}), f32[512,256]{1,0:T(8,128)}) %reduce-scatter.3.cloned.1.call-update) | async-done | bytes 524304 | tf_op jit(solution)/shard_map/reduce_scatter | solution.py:124
  291.3 4.3 %fusion.5 = bf16[512,256]{1,0:T(8,128)(2,1)} fusion(f32[512,256]{1,0:T(8,128)} %reduce-scatter.3.cloned.1.call-done, bf16[512,4096]{0,1:T(8,128)(2,1)} %bitcast.139, bf16[4096,256]{1,0:T(8,128)(2,1)S(1)} %bitcast.140), kind=kOutput, calls=%fused_computation.21 | convolution fusion | flops 1074003968 | bytes 7077888 | tf_op jit(solution)/shard_map/dot_general | solution.py:157
  (74 shorter events, 17.9 us)
Async XLA Ops:
  6.5 185.9 %copy-start = (bf16[1024,256]{1,0:T(8,128)(2,1)S(1)}, bf16[1024,256]{1,0:T(8,128)(2,1)}, u32[]{:S(2)}) copy-start(bf16[1024,256]{1,0:T(8,128)(2,1)} %param.19) | copy-start | bytes 1572868
  6.5 32.4 %copy-start.2 = (s32[32]{0:T(128)S(1)}, s32[32]{0:T(128)}, u32[]{:S(2)}) copy-start(s32[32]{0:T(128)} %param.14) | copy-start | bytes 388
  6.5 136.7 %all-gather.5.cloned.1.call-start = ((), (), s32[]{:S(2)}) async-start(), calls=%async_computation.8 | async-start | bytes 8650752 | tf_op jit(solution)/shard_map/all_gather | solution.py:130
  11.2 20.1 %all-to-all-start = ((s32[32,2,1]{1,2,0:T(1,128)}), s32[32,2,1]{1,2,0:T(1,128)S(1)}, u32[]{:S(2)}, u32[]{:S(2)}) async-start(s32[32,2,1]{1,2,0:T(1,128)} %bitcast.3), calls=%async_computation | async-start | bytes 32768 | tf_op jit(solution)/shard_map/all_to_all | solution.py:36
  31.3 24.5 %all-to-all-start.1 = ((bf16[64,32,2,128]{3,2,1,0:T(2,128)(2,1)}), bf16[64,32,2,128]{3,2,1,0:T(2,128)(2,1)S(1)}, u32[]{:S(2)}, u32[]{:S(2)}) async-start(bf16[64,32,2,128]{3,2,1,0:T(2,128)(2,1)} %broadcast_select_fusion.2), calls=%async_computation.1 | async-start | bytes 2097152 | tf_op jit(solution)/shard_map/all_to_all | solution.py:35
  38.7 153.7 %all-gather.3.cloned.1.call-start = ((), (), s32[]{:S(2)}) async-start(), calls=%async_computation.6 | async-start | bytes 8650752 | tf_op jit(solution)/shard_map/all_gather | solution.py:116
  127.8 2.4 copy-start.5
  127.8 3.5 %copy-start.4 = (s32[32]{0:T(128)S(1)}, s32[32]{0:T(128)}, u32[]{:S(2)}) copy-start(s32[32]{0:T(128)} %param.15) | copy-start | bytes 388
  127.8 14.8 %copy-start.3 = (s32[64]{0:T(128)S(1)}, s32[64]{0:T(128)}, u32[]{:S(2)}) copy-start(s32[64]{0:T(128)} %param.16) | copy-start | bytes 772
  130.1 134.3 %reduce-scatter.5.cloned.1.call-start = ((), (), s32[]{:S(2)}) async-start(), calls=%async_computation.9 | async-start | bytes 1179648 | tf_op jit(solution)/shard_map/reduce_scatter | solution.py:145
  175.8 115.5 %reduce-scatter.3.cloned.1.call-start = ((), (), s32[]{:S(2)}) async-start(), calls=%async_computation.7 | async-start | bytes 4718592 | tf_op jit(solution)/shard_map/reduce_scatter | solution.py:124
  200.1 1.6 copy-start.1
  218.4 32.6 %all-to-all-start.3 = ((bf16[32,2,16384]{2,1,0:T(2,128)(2,1)}), bf16[32,2,16384]{2,1,0:T(2,128)(2,1)S(1)}, u32[]{:S(2)}, u32[]{:S(2)}) async-start(bf16[32,2,16384]{2,1,0:T(2,128)(2,1)} %reshape.337), calls=%async_computation.5 | async-start | bytes 4194304 | tf_op jit(solution)/shard_map/all_to_all | solution.py:146
Sparse Core Ops, SparseCore 0:
  9.9 63.9 all-gather.4
  130.2 62.1 all-gather.2
  194.9 35.2 reduce-scatter.4
  232.7 58.6 reduce-scatter.2
